TPU v7x, 128 devices: a whole 4x4x4 slice. The times are simulated.
128 devices in a mesh: blk: 8 (over x_lo, y), row: 16 (over x_hi, z, core).
Axes of the slice: x: 4 (x_hi: 2, x_lo: 2; x = x_hi * 2 + x_lo), y: 4, z: 4, core: 2. Of those that a mesh axis runs over, the one named last changes fastest.
Arguments:
- intersection: bfloat16 [4096, 4096], P('row', 'blk'), may hold values from -0.09375 to 0.09375
- inverse_dev: bfloat16 [4096, 4096], P('row', 'blk'), may hold values from -0.09375 to 0.09375
- hamiltonian: bfloat16 [4096, 4096], P('row', 'blk'), may hold values from -0.0625 to 0.0625
- chem_potential: float32 [1], replicated, may hold values from -0.4 to 0.4
- pattern_s: int32 [32, 32], replicated, may hold values 0 or 1
- pattern_z: int32 [32, 32], replicated, may hold values 0 or 1
- pattern_h: int32 [32, 32], replicated, may hold values 0 or 1
- fill_inverse: int32 [32, 32], replicated, may hold values 0 or 1
- fill_sign: int32 [32, 32], replicated, may hold values 0 or 1
Outputs:
- refined_inverse: bfloat16 [4096, 4096], P('row', 'blk')
- inverse_error: bfloat16 [4096, 4096], P('row', 'blk')
- sign_step: bfloat16 [4096, 4096], P('row', 'blk')
All inputs are finite; a program needn't handle non-finite values.
Results may differ from a plain program's by a relative error of at most 0.0067.
Values may be sent and summed in bfloat16 or wider, within the bound.
No kernel may reach another device: no remote copies, remote signals or barrier semaphores. Data moves between devices by JAX's collectives and lax.ppermute only.
A program may use at most 64 MiB of HBM per device.

v0:
```python
import jax
import jax.numpy as jnp
from jax import lax
from jax.sharding import PartitionSpec as P

BS = 128


def expand_local(pattern, row_start, rows, col_start, cols):
    count = pattern.shape[0]
    labels = jnp.arange(count, dtype=jnp.int32)
    row_blocks = (row_start + jnp.arange(rows, dtype=jnp.int32)) // BS
    col_blocks = (col_start + jnp.arange(cols, dtype=jnp.int32)) // BS
    row_pick = (row_blocks[:, None] == labels[None, :]).astype(jnp.float32)
    col_pick = (col_blocks[:, None] == labels[None, :]).astype(jnp.float32)
    inner = jnp.dot(row_pick, pattern.astype(jnp.float32), precision=lax.Precision.HIGHEST)
    return jnp.dot(inner, col_pick.T, precision=lax.Precision.HIGHEST)


def make_folder(panel, piece):
    return jnp.dot(panel, piece, preferred_element_type=jnp.float32)


def body(
    intersection,
    inverse_dev,
    hamiltonian,
    chem_potential,
    pattern_s,
    pattern_z,
    pattern_h,
    fill_inverse,
    fill_sign,
):
    rows, cols = intersection.shape
    row_start = lax.axis_index("row") * rows
    col_start = lax.axis_index("blk") * cols
    ident = (
        (row_start + jnp.arange(rows, dtype=jnp.int32))[:, None]
        == (col_start + jnp.arange(cols, dtype=jnp.int32))[None, :]
    ).astype(jnp.float32)
    seff = (
        ident
        + 0.35
        * expand_local(pattern_s, row_start, rows, col_start, cols)
        * intersection.astype(jnp.float32)
    ).astype(jnp.bfloat16)
    zeff = (
        ident
        - 0.35
        * expand_local(pattern_z, row_start, rows, col_start, cols)
        * inverse_dev.astype(jnp.float32)
    ).astype(jnp.bfloat16)
    heff = (
        expand_local(pattern_h, row_start, rows, col_start, cols) * hamiltonian.astype(jnp.float32)
    ).astype(jnp.bfloat16)
    z_rows = lax.all_gather(zeff, "blk", axis=1, tiled=True)
    s_cols = lax.all_gather(seff, "row", axis=0, tiled=True)
    first = jnp.dot(z_rows, s_cols, preferred_element_type=jnp.float32).astype(jnp.bfloat16)
    f_rows = lax.all_gather(first, "blk", axis=1, tiled=True)
    second = make_folder(f_rows, lax.all_gather(zeff, "row", axis=0, tiled=True))
    keep_inverse = expand_local(fill_inverse, row_start, rows, col_start, cols)
    refined = (keep_inverse * (2.0 * zeff.astype(jnp.float32) - second)).astype(jnp.bfloat16)
    r_rows = lax.all_gather(refined, "blk", axis=1, tiled=True)
    error = (ident - jnp.dot(r_rows, s_cols, preferred_element_type=jnp.float32)).astype(
        jnp.bfloat16
    )
    third = make_folder(r_rows, lax.all_gather(heff, "row", axis=0, tiled=True))
    keep_sign = expand_local(fill_sign, row_start, rows, col_start, cols)
    shifted = (keep_sign * third - chem_potential[0] * ident).astype(jnp.bfloat16)
    x_rows = lax.all_gather(shifted, "blk", axis=1, tiled=True)
    squared = make_folder(x_rows, lax.all_gather(shifted, "row", axis=0, tiled=True))
    square = (keep_sign * squared).astype(jnp.bfloat16)
    cube = make_folder(x_rows, lax.all_gather(square, "row", axis=0, tiled=True))
    sign = (0.5 * (3.0 * shifted.astype(jnp.float32) - cube)).astype(jnp.bfloat16)
    return (refined, error, sign)


def solution(mesh):
    placed = (P("row", "blk"), P("row", "blk"), P("row", "blk"), P(), P(), P(), P(), P(), P())
    return jax.shard_map(
        body,
        mesh=mesh,
        in_specs=placed,
        out_specs=(P("row", "blk"), P("row", "blk"), P("row", "blk")),
        check_vma=False,
    )
```

profile of v0, /device:TPU:1, one launch (start us, length us, event | category | flops | bytes accessed | tf_op | source)
XLA Modules:
  0.0 479.5 jit_solution(4841761674206644709)
XLA Ops:
  7.3 1.0 fusion.23
  8.3 2.2 fusion.10
  10.5 0.0 all-gather.12.cloned.1.call-start
  10.5 1.0 fusion.22
  11.5 2.2 fusion.9
  13.7 0.0 all-gather.16.cloned.1.call-start
  13.8 0.7 all-gather.16.cloned.1.call-update
  14.5 35.2 %all-gather.10.cloned.1.call-done = bf16[256,4096]{1,0:T(8,128)(2,1)} async-done(((bf16[256,512]{1,0:T(8,128)(2,1)}), bf16[256,4096]{1,0:T(8,128)(2,1)}) %all-gather.10.cloned.1.call-update) | async-done | bytes 2097168 | tf_op jit(solution)/shard_map/all_gather | solution.py:57
  49.7 63.2 %all-gather.12.cloned.1.call-done = bf16[4096,512]{1,0:T(8,128)(2,1)} async-done(((bf16[256,512]{1,0:T(8,128)(2,1)}), bf16[4096,512]{1,0:T(8,128)(2,1)}) %all-gather.12.cloned.1.call-update) | async-done | bytes 4194320 | tf_op jit(solution)/shard_map/all_gather | solution.py:58
  112.9 4.8 convolution_convert_fusion
  117.7 0.0 all-gather.20.cloned.1.call-start
  117.8 0.3 fusion.20
  118.0 1.2 fusion.12
  119.3 0.0 all-gather.18.cloned.1.call-start
  119.3 0.3 fusion.24
  119.6 49.1 %all-gather.16.cloned.1.call-done = bf16[4096,512]{1,0:T(8,128)(2,1)} async-done(((bf16[256,512]{1,0:T(8,128)(2,1)}), bf16[4096,512]{1,0:T(8,128)(2,1)}) %all-gather.16.cloned.1.call-update) | async-done | bytes 4194320 | tf_op jit(solution)/shard_map/all_gather | solution.py:61
  168.7 35.3 %all-gather.14.cloned.1.call-done = bf16[256,4096]{1,0:T(8,128)(2,1)} async-done(((bf16[256,512]{1,0:T(8,128)(2,1)}), bf16[256,4096]{1,0:T(8,128)(2,1)}) %all-gather.14.cloned.1.call-update) | async-done | bytes 2097168 | tf_op jit(solution)/shard_map/all_gather | solution.py:60
  204.0 4.1 convolution_subtract_fusion.2
  208.1 1.2 fusion.11
  209.3 0.0 all-gather.22.cloned.1.call-start
  210.0 0.3 fusion.21
  210.3 0.5 fusion.14
  210.8 55.7 %all-gather.20.cloned.1.call-done = bf16[4096,512]{1,0:T(8,128)(2,1)} async-done(((bf16[256,512]{1,0:T(8,128)(2,1)}), bf16[4096,512]{1,0:T(8,128)(2,1)}) %all-gather.20.cloned.1.call-update) | async-done | bytes 4194320 | tf_op jit(solution)/shard_map/all_gather | solution.py:68
  266.5 35.3 %all-gather.18.cloned.1.call-done = bf16[256,4096]{1,0:T(8,128)(2,1)} async-done(((bf16[256,512]{1,0:T(8,128)(2,1)}), bf16[256,4096]{1,0:T(8,128)(2,1)}) %all-gather.18.cloned.1.call-update) | async-done | bytes 2097168 | tf_op jit(solution)/shard_map/all_gather | solution.py:64
  301.8 4.8 fusion.6
  306.7 0.7 all-gather.24.cloned.1.call-update
  307.4 40.0 %all-gather.22.cloned.1.call-done = bf16[256,4096]{1,0:T(8,128)(2,1)} async-done(((bf16[256,512]{1,0:T(8,128)(2,1)}), bf16[256,4096]{1,0:T(8,128)(2,1)}) %all-gather.22.cloned.1.call-update) | async-done | bytes 2097168 | tf_op jit(solution)/shard_map/all_gather | solution.py:71
  347.4 63.2 %all-gather.24.cloned.1.call-done = bf16[4096,512]{1,0:T(8,128)(2,1)} async-done(((bf16[256,512]{1,0:T(8,128)(2,1)}), bf16[4096,512]{1,0:T(8,128)(2,1)}) %all-gather.24.cloned.1.call-update) | async-done | bytes 4194320 | tf_op jit(solution)/shard_map/all_gather | solution.py:72
  410.5 4.8 fusion.13
  415.4 4.2 fusion.7
  419.6 48.6 %all-gather.26.cloned.1.call-done = bf16[4096,512]{1,0:T(8,128)(2,1)} async-done(((bf16[256,512]{1,0:T(8,128)(2,1)}), bf16[4096,512]{1,0:T(8,128)(2,1)}) %all-gather.26.cloned.1.call-update) | async-done | bytes 4194320 | tf_op jit(solution)/shard_map/all_gather | solution.py:74
  468.2 4.8 fusion.8
  (29 shorter events, 0.3 us)
Async XLA Ops:
  7.2 42.6 %all-gather.10.cloned.1.call-start = ((), (), s32[]{:S(2)}) async-start(), calls=%async_computation | async-start | bytes 2359296 | tf_op jit(solution)/shard_map/all_gather | solution.py:57
  10.5 102.4 %all-gather.12.cloned.1.call-start = ((), (), s32[]{:S(2)}) async-start(), calls=%async_computation.1 | async-start | bytes 4456448 | tf_op jit(solution)/shard_map/all_gather | solution.py:58
  13.7 104.0 %copy-start.3 = (s32[32,32]{1,0:T(8,128)S(1)}, s32[32,32]{1,0:T(8,128)}, u32[]{:S(2)}) copy-start(s32[32,32]{1,0:T(8,128)} %param.15) | copy-start | bytes 12292
  13.7 104.3 %copy-start.2 = (bf16[256,512]{1,0:T(8,128)(2,1)S(1)}, bf16[256,512]{1,0:T(8,128)(2,1)}, u32[]{:S(2)}) copy-start(bf16[256,512]{1,0:T(8,128)(2,1)} %param.11) | copy-start | bytes 786436
  13.7 155.0 %all-gather.16.cloned.1.call-start = ((), (), s32[]{:S(2)}) async-start(), calls=%async_computation.3 | async-start | bytes 4456448 | tf_op jit(solution)/shard_map/all_gather | solution.py:61
  14.5 104.9 %copy-start.4 = (s32[32,32]{1,0:T(8,128)S(1)}, s32[32,32]{1,0:T(8,128)}, u32[]{:S(2)}) copy-start(s32[32,32]{1,0:T(8,128)} %param.16) | copy-start | bytes 12292
  14.5 189.5 %copy-start = (bf16[256,512]{1,0:T(8,128)(2,1)S(1)}, bf16[256,512]{1,0:T(8,128)(2,1)}, u32[]{:S(2)}) copy-start(bf16[256,512]{1,0:T(8,128)(2,1)} %fusion.10) | copy-start | bytes 786436
  14.5 189.5 %all-gather.14.cloned.1.call-start = ((), (), s32[]{:S(2)}) async-start(), calls=%async_computation.2 | async-start | bytes 2359296 | tf_op jit(solution)/shard_map/all_gather | solution.py:60
  117.7 148.8 %all-gather.20.cloned.1.call-start = ((), (), s32[]{:S(2)}) async-start(), calls=%async_computation.5 | async-start | bytes 4456448 | tf_op jit(solution)/shard_map/all_gather | solution.py:68
  119.3 182.5 %all-gather.18.cloned.1.call-start = ((), (), s32[]{:S(2)}) async-start(), calls=%async_computation.4 | async-start | bytes 2359296 | tf_op jit(solution)/shard_map/all_gather | solution.py:64
  119.6 90.4 %copy-start.5 = (s32[32,32]{1,0:T(8,128)S(1)}, s32[32,32]{1,0:T(8,128)}, u32[]{:S(2)}) copy-start(s32[32,32]{1,0:T(8,128)} %param.17) | copy-start | bytes 12292
  209.3 138.1 %all-gather.22.cloned.1.call-start = ((), (), s32[]{:S(2)}) async-start(), calls=%async_computation.6 | async-start | bytes 2359296 | tf_op jit(solution)/shard_map/all_gather | solution.py:71
  306.6 108.8 %copy-start.6 = (bf16[256,4096]{1,0:T(8,128)(2,1)S(1)}, bf16[256,4096]{1,0:T(8,128)(2,1)}, u32[]{:S(2)}) copy-start(bf16[256,4096]{1,0:T(8,128)(2,1)} %all-gather.18.cloned.1.call-done) | copy-start | bytes 6291460
  306.6 103.9 %all-gather.24.cloned.1.call-start = ((), (), s32[]{:S(2)}) async-start(), calls=%async_computation.7 | async-start | bytes 4456448 | tf_op jit(solution)/shard_map/all_gather | solution.py:72
  307.4 160.9 %all-gather.26.cloned.1.call-start = ((), (), s32[]{:S(2)}) async-start(), calls=%async_computation.8 | async-start | bytes 4456448 | tf_op jit(solution)/shard_map/all_gather | solution.py:74
  415.3 52.9 %copy-start.1 = (bf16[256,512]{1,0:T(8,128)(2,1)S(1)}, bf16[256,512]{1,0:T(8,128)(2,1)}, u32[]{:S(2)}) copy-start(bf16[256,512]{1,0:T(8,128)(2,1)} %fusion.6) | copy-start | bytes 786436
Sparse Core Ops, SparseCore 0:
  10.6 39.0 all-gather.9
  52.8 60.0 all-gather.11
  115.9 52.6 all-gather.15
  170.8 33.2 all-gather.13
  206.3 60.0 all-gather.19
  268.5 33.2 all-gather.17
  306.7 40.6 all-gather.21
  350.4 60.0 all-gather.23
  415.5 52.6 all-gather.25
where the time goes:
time: 480 us
  waiting for transfers between devices  427 us (89%)
  matrix products  37.4 us (8%)
  between operations  14.7 us (3%)
    all_gather x1, waiting for transfers between devices, body(): s_cols = lax.all_gather(seff, 'row', axis=0, tiled=True)  63.2 us
    all_gather x1, waiting for transfers between devices, body(): lax.all_gather(shifted, 'row', axis=0, tiled=True)  63.2 us
    all_gather x1, waiting for transfers between devices, body(): third = make_folder(r_rows, lax.all_gather(heff, 'row', axis=0, tiled=True))  55.7 us
    all_gather x1, waiting for transfers between devices, body(): lax.all_gather(zeff, 'row', axis=0, tiled=True)  49.1 us
    all_gather x1, waiting for transfers between devices, body(): lax.all_gather(square, 'row', axis=0, tiled=True)  48.6 us
    all_gather x1, waiting for transfers between devices, body(): x_rows = lax.all_gather(shifted, 'blk', axis=1, tiled=True)  40 us
    all_gather x1, waiting for transfers between devices, body(): f_rows = lax.all_gather(first, 'blk', axis=1, tiled=True)  35.3 us
    all_gather x1, waiting for transfers between devices, body(): r_rows = lax.all_gather(refined, 'blk', axis=1, tiled=True)  35.3 us
  transfers between devices with their start and end apart: 9, of which 9 were waited for; matrix products, arithmetic and copies ran while one was open for 4% of the time, Pallas kernels for 0%

commit v1 on v0

--- a/solution.py
+++ b/solution.py
@@ -57,7 +57,9 @@
     z_rows = lax.all_gather(zeff, "blk", axis=1, tiled=True)
     s_cols = lax.all_gather(seff, "row", axis=0, tiled=True)
     first = jnp.dot(z_rows, s_cols, preferred_element_type=jnp.float32).astype(jnp.bfloat16)
-    f_rows = lax.all_gather(first, "blk", axis=1, tiled=True)
+    f_rows = jnp.concatenate(
+        lax.all_to_all(jnp.stack([first for _ in range(lax.axis_size("blk"))]), "blk", 0, 0), axis=1
+    )
     second = make_folder(f_rows, lax.all_gather(zeff, "row", axis=0, tiled=True))
     keep_inverse = expand_local(fill_inverse, row_start, rows, col_start, cols)
     refined = (keep_inverse * (2.0 * zeff.astype(jnp.float32) - second)).astype(jnp.bfloat16)

time: 480 us -> 441 us (0.919)
  waiting for transfers between devices: 427 us -> 381 us
    all_gather x1 -> x0, waiting for transfers between devices: 35.3 us -> none  [body(): f_rows = lax.all_gather(first, 'blk', axis=1, tiled=True)]
    all_gather x1, waiting for transfers between devices: 55.7 us -> 48.9 us  [body(): third = make_folder(r_rows, lax.all_gather(heff, 'row', axis=0, tiled=True))]
  transfers between devices with their start and end apart: 9 -> 9, of which waited for: 9 -> 8; matrix products, arithmetic and copies ran while one was open for 4% -> 5% of each run, Pallas kernels for 0% -> 0%
where the time goes in v1:
time: 441 us; the launch traced here: 440 us
  waiting for transfers between devices  381 us (86%)
  matrix products  37.8 us (9%)
  between operations  14.9 us (3%)
    all_gather x1, waiting for transfers between devices, body(): s_cols = lax.all_gather(seff, 'row', axis=0, tiled=True)  63.2 us
    all_gather x1, waiting for transfers between devices, body(): lax.all_gather(shifted, 'row', axis=0, tiled=True)  63.2 us
    all_gather x1, waiting for transfers between devices, body(): third = make_folder(r_rows, lax.all_gather(heff, 'row', axis=0, tiled=True))  48.9 us
    all_gather x1, waiting for transfers between devices, body(): lax.all_gather(zeff, 'row', axis=0, tiled=True)  48.8 us
    all_gather x1, waiting for transfers between devices, body(): lax.all_gather(square, 'row', axis=0, tiled=True)  48.6 us
    all_gather x1, waiting for transfers between devices, body(): x_rows = lax.all_gather(shifted, 'blk', axis=1, tiled=True)  40 us
    all_gather x1, waiting for transfers between devices, body(): r_rows = lax.all_gather(refined, 'blk', axis=1, tiled=True)  35.3 us
    all_gather x1, waiting for transfers between devices, body(): z_rows = lax.all_gather(zeff, 'blk', axis=1, tiled=True)  32 us
  transfers between devices with their start and end apart: 9, of which 8 were waited for; matrix products, arithmetic and copies ran while one was open for 5% of the time, Pallas kernels for 0%

profile of v1, /device:TPU:1, one launch (start us, length us, event | category | flops | bytes accessed | tf_op | source)
XLA Modules:
  0.0 440.1 jit_solution(10017777731580842221)
XLA Ops:
  7.3 1.0 fusion.23
  8.3 2.2 fusion.10
  10.5 0.0 all-gather.11.cloned.1.call-start
  10.5 1.0 fusion.22
  11.5 2.2 fusion.9
  13.7 0.0 all-gather.13.cloned.1.call-start
  13.8 0.7 all-gather.13.cloned.1.call-update
  14.5 1.0 fusion.20
  15.5 2.2 fusion.12
  17.7 32.0 %all-gather.9.cloned.1.call-done = bf16[256,4096]{1,0:T(8,128)(2,1)} async-done(((bf16[256,512]{1,0:T(8,128)(2,1)}), bf16[256,4096]{1,0:T(8,128)(2,1)}) %all-gather.9.cloned.1.call-update) | async-done | bytes 2097168 | tf_op jit(solution)/shard_map/all_gather | solution.py:57
  49.7 63.2 %all-gather.11.cloned.1.call-done = bf16[4096,512]{1,0:T(8,128)(2,1)} async-done(((bf16[256,512]{1,0:T(8,128)(2,1)}), bf16[4096,512]{1,0:T(8,128)(2,1)}) %all-gather.11.cloned.1.call-update) | async-done | bytes 4194320 | tf_op jit(solution)/shard_map/all_gather | solution.py:58
  112.9 4.1 convolution_convert_fusion
  117.0 0.1 copy.12
  117.1 1.4 stack.2
  118.6 4.0 all-to-all-start
  122.6 0.3 fusion.24
  122.9 48.8 %all-gather.13.cloned.1.call-done = bf16[4096,512]{1,0:T(8,128)(2,1)} async-done(((bf16[256,512]{1,0:T(8,128)(2,1)}), bf16[4096,512]{1,0:T(8,128)(2,1)}) %all-gather.13.cloned.1.call-update) | async-done | bytes 4194320 | tf_op jit(solution)/shard_map/all_gather | solution.py:63
  171.7 3.5 convolution_subtract_fusion.2
  175.2 1.2 fusion.11
  176.4 0.0 all-gather.19.cloned.1.call-start
  177.1 0.3 fusion.21
  177.4 0.5 fusion.14
  177.8 48.9 %all-gather.17.cloned.1.call-done = bf16[4096,512]{1,0:T(8,128)(2,1)} async-done(((bf16[256,512]{1,0:T(8,128)(2,1)}), bf16[4096,512]{1,0:T(8,128)(2,1)}) %all-gather.17.cloned.1.call-update) | async-done | bytes 4194320 | tf_op jit(solution)/shard_map/all_gather | solution.py:70
  226.7 35.3 %all-gather.15.cloned.1.call-done = bf16[256,4096]{1,0:T(8,128)(2,1)} async-done(((bf16[256,512]{1,0:T(8,128)(2,1)}), bf16[256,4096]{1,0:T(8,128)(2,1)}) %all-gather.15.cloned.1.call-update) | async-done | bytes 2097168 | tf_op jit(solution)/shard_map/all_gather | solution.py:66
  262.1 4.8 %fusion.6 = bf16[256,512]{1,0:T(8,128)(2,1)} fusion(f32[256,512]{1,0:T(8,128)S(1)} %fusion.14, bf16[256,4096]{1,0:T(8,128)(2,1)} %all-gather.15.cloned.1.call-done, bf16[4096,512]{1,0:T(8,128)(2,1)} %all-gather.17.cloned.1.call-done, f32[]{:T(128)} %bitcast.21, s32[512]{0:T(512)S(1)} %iota_add_fusion, s32[256]{0:T(256)S(1)} %iota_add_fusion.1), kind=kOutput, calls=%fused_computation.15 | convolution fusion | flops 1074397184 | bytes 7080964 | tf_op jit(solution)/shard_map/dot_general | solution.py:21
  266.9 0.7 all-gather.21.cloned.1.call-update
  267.7 40.0 %all-gather.19.cloned.1.call-done = bf16[256,4096]{1,0:T(8,128)(2,1)} async-done(((bf16[256,512]{1,0:T(8,128)(2,1)}), bf16[256,4096]{1,0:T(8,128)(2,1)}) %all-gather.19.cloned.1.call-update) | async-done | bytes 2097168 | tf_op jit(solution)/shard_map/all_gather | solution.py:73
  307.6 63.2 %all-gather.21.cloned.1.call-done = bf16[4096,512]{1,0:T(8,128)(2,1)} async-done(((bf16[256,512]{1,0:T(8,128)(2,1)}), bf16[4096,512]{1,0:T(8,128)(2,1)}) %all-gather.21.cloned.1.call-update) | async-done | bytes 4194320 | tf_op jit(solution)/shard_map/all_gather | solution.py:74
  370.8 4.8 %fusion.13 = bf16[256,512]{1,0:T(8,128)(2,1)} fusion(f32[256,512]{1,0:T(8,128)S(1)} %fusion.14, bf16[256,4096]{1,0:T(8,128)(2,1)} %all-gather.19.cloned.1.call-done, bf16[4096,512]{1,0:T(8,128)(2,1)} %all-gather.21.cloned.1.call-done), kind=kOutput, calls=%fused_computation.22 | convolution fusion | flops 1074003968 | bytes 7077888 | tf_op jit(solution)/shard_map/dot_general | solution.py:21
  375.6 4.2 fusion.7
  379.9 48.6 %all-gather.23.cloned.1.call-done = bf16[4096,512]{1,0:T(8,128)(2,1)} async-done(((bf16[256,512]{1,0:T(8,128)(2,1)}), bf16[4096,512]{1,0:T(8,128)(2,1)}) %all-gather.23.cloned.1.call-update) | async-done | bytes 4194320 | tf_op jit(solution)/shard_map/all_gather | solution.py:76
  428.5 4.8 %fusion.8 = bf16[256,512]{1,0:T(8,128)(2,1)} fusion(bf16[256,4096]{1,0:T(8,128)(2,1)} %all-gather.19.cloned.1.call-done, bf16[4096,512]{1,0:T(8,128)(2,1)} %all-gather.23.cloned.1.call-done, bf16[256,512]{1,0:T(8,128)(2,1)S(1)} %copy-done.1), kind=kOutput, calls=%fused_computation.17 | convolution fusion | flops 1074397184 | bytes 6815744 | tf_op jit(solution)/shard_map/dot_general | solution.py:21
  (26 shorter events, 0.4 us)
Async XLA Ops:
  7.2 42.6 %all-gather.9.cloned.1.call-start = ((), (), s32[]{:S(2)}) async-start(), calls=%async_computation.1 | async-start | bytes 2359296 | tf_op jit(solution)/shard_map/all_gather | solution.py:57
  10.5 102.4 %all-gather.11.cloned.1.call-start = ((), (), s32[]{:S(2)}) async-start(), calls=%async_computation.2 | async-start | bytes 4456448 | tf_op jit(solution)/shard_map/all_gather | solution.py:58
  13.7 158.0 %all-gather.13.cloned.1.call-start = ((), (), s32[]{:S(2)}) async-start(), calls=%async_computation.3 | async-start | bytes 4456448 | tf_op jit(solution)/shard_map/all_gather | solution.py:63
  14.5 212.3 %all-gather.17.cloned.1.call-start = ((), (), s32[]{:S(2)}) async-start(), calls=%async_computation.5 | async-start | bytes 4456448 | tf_op jit(solution)/shard_map/all_gather | solution.py:70
  117.0 5.7 %copy-start.2 = (s32[32,32]{1,0:T(8,128)S(1)}, s32[32,32]{1,0:T(8,128)}, u32[]{:S(2)}) copy-start(s32[32,32]{1,0:T(8,128)} %param.16) | copy-start | bytes 12292
  117.0 54.7 %copy-start = (bf16[256,512]{1,0:T(8,128)(2,1)S(1)}, bf16[256,512]{1,0:T(8,128)(2,1)}, u32[]{:S(2)}) copy-start(bf16[256,512]{1,0:T(8,128)(2,1)} %fusion.10) | copy-start | bytes 786436
  118.6 53.1 %all-to-all-start = ((bf16[8,256,512]{1,2,0:T(8,128)(2,1)}), bf16[8,256,512]{1,2,0:T(8,128)(2,1)S(1)}, u32[]{:S(2)}, u32[]{:S(2)}) async-start(bf16[8,256,512]{1,2,0:T(8,128)(2,1)} %stack.2), calls=%async_computation | async-start | bytes 4194304 | tf_op jit(solution)/shard_map/all_to_all | solution.py:61
  122.6 139.5 %all-gather.15.cloned.1.call-start = ((), (), s32[]{:S(2)}) async-start(), calls=%async_computation.4 | async-start | bytes 2359296 | tf_op jit(solution)/shard_map/all_gather | solution.py:66
  171.7 5.4 %copy-start.3 = (s32[32,32]{1,0:T(8,128)S(1)}, s32[32,32]{1,0:T(8,128)}, u32[]{:S(2)}) copy-start(s32[32,32]{1,0:T(8,128)} %param.17) | copy-start | bytes 12292
  176.4 131.3 %all-gather.19.cloned.1.call-start = ((), (), s32[]{:S(2)}) async-start(), calls=%async_computation.6 | async-start | bytes 2359296 | tf_op jit(solution)/shard_map/all_gather | solution.py:73
  266.8 108.8 %copy-start.4 = (bf16[256,4096]{1,0:T(8,128)(2,1)S(1)}, bf16[256,4096]{1,0:T(8,128)(2,1)}, u32[]{:S(2)}) copy-start(bf16[256,4096]{1,0:T(8,128)(2,1)} %all-gather.15.cloned.1.call-done) | copy-start | bytes 6291460
  266.9 103.9 %all-gather.21.cloned.1.call-start = ((), (), s32[]{:S(2)}) async-start(), calls=%async_computation.7 | async-start | bytes 4456448 | tf_op jit(solution)/shard_map/all_gather | solution.py:74
  267.6 160.9 %all-gather.23.cloned.1.call-start = ((), (), s32[]{:S(2)}) async-start(), calls=%async_computation.8 | async-start | bytes 4456448 | tf_op jit(solution)/shard_map/all_gather | solution.py:76
  375.6 52.9 %copy-start.1 = (bf16[256,512]{1,0:T(8,128)(2,1)S(1)}, bf16[256,512]{1,0:T(8,128)(2,1)}, u32[]{:S(2)}) copy-start(bf16[256,512]{1,0:T(8,128)(2,1)} %fusion.6) | copy-start | bytes 786436
Sparse Core Ops, SparseCore 0:
  10.6 39.0 all-gather.8
  52.8 60.0 all-gather.10
  115.9 55.6 all-gather.12
  174.0 52.6 all-gather.16
  228.8 33.2 all-gather.14
  267.0 40.5 all-gather.18
  310.7 60.0 all-gather.20
  375.7 52.6 all-gather.22
